TPU v7x, 32 devices: a whole 2x2x4 slice. The times are simulated.
32 devices in a mesh: batch: 8 (over y, x, core), chan: 4 (over z).
Axes of the slice: x: 2, y: 2, z: 4, core: 2. Of those that a mesh axis runs over, the one named last changes fastest.
Arguments:
- fine_inputs: bfloat16 [8, 32, 32, 512], P('batch'), may hold values from -6 to 6
- fine_upstream: bfloat16 [8, 32, 32, 512], P('batch', None, None, 'chan'), may hold values from -6 to 6
- fine_bank: bfloat16 [8, 9, 512, 512], P(None, None, 'batch', 'chan'), may hold values from -0.09375 to 0.09375
- fine_coefs: float32 [8, 8], replicated, may hold values from 0 to 1, as said below
- coarse_inputs: bfloat16 [8, 16, 16, 512], P('batch'), may hold values from -6 to 6
- coarse_upstream: bfloat16 [8, 16, 16, 512], P('batch', None, None, 'chan'), may hold values from -6 to 6
- coarse_bank: bfloat16 [8, 9, 512, 512], P(None, None, 'batch', 'chan'), may hold values from -0.09375 to 0.09375
- coarse_coefs: float32 [8, 8], replicated, may hold values from 0 to 1, as said below
Outputs:
- fine_delta: bfloat16 [8, 32, 32, 512], P('batch', None, None, 'chan')
- fine_update: float32 [8, 9, 512, 512], P(None, None, 'batch', 'chan')
- fine_logit: float32 [8, 8], P('batch')
- coarse_delta: bfloat16 [8, 16, 16, 512], P('batch', None, None, 'chan')
- coarse_update: float32 [8, 9, 512, 512], P(None, None, 'batch', 'chan')
- coarse_logit: float32 [8, 8], P('batch')
Inputs may be any that keep to these rules, and one draw needn't show every extreme that they name: Each row of fine_coefs is a softmax: positive entries that sum to one. Each row of coarse_coefs is a softmax: positive entries that sum to one.
All inputs are finite; a program needn't handle non-finite values.
Results may differ from a plain program's by a relative error of at most 0.01.
Values may be sent and summed in bfloat16 or wider, within the bound.
No kernel may reach another device: no remote copies, remote signals or barrier semaphores. Data moves between devices by JAX's collectives and lax.ppermute only.
A program may use at most 128 MiB of HBM per device.

v0:
```python
import jax
import jax.numpy as jnp
from jax import lax
from jax.sharding import PartitionSpec as P

BANKS = 8
FINE_SIDE = 32
COARSE_SIDE = 16
HIGH = lax.Precision.HIGHEST


def shifted(padded, row_shift, col_shift, side):
    window = padded[:, row_shift : row_shift + side, col_shift : col_shift + side, :]
    return window.reshape(window.shape[0], side * side, window.shape[3])


def local_grads(inputs, upstream, kernels, side):
    samples_here = inputs.shape[0]
    pad_in = jnp.pad(inputs, ((0, 0), (1, 1), (1, 1), (0, 0)))
    pad_up = jnp.pad(upstream, ((0, 0), (1, 1), (1, 1), (0, 0)))
    flat_up = upstream.reshape(samples_here, side * side, upstream.shape[3])
    delta = jnp.zeros((samples_here, side * side, inputs.shape[3]), jnp.float32)
    grad_taps = []
    for row_shift in range(3):
        for col_shift in range(3):
            tap = 3 * row_shift + col_shift
            window_in = shifted(pad_in, row_shift, col_shift, side)
            window_up = shifted(pad_up, 2 - row_shift, 2 - col_shift, side)
            grad_taps.append(
                jnp.einsum("bpc,bpo->bco", window_in, flat_up, preferred_element_type=jnp.float32)
                / side
            )
            delta = delta + jnp.einsum(
                "bpo,bco->bpc", window_up, kernels[:, tap], preferred_element_type=jnp.float32
            )
    return (delta.reshape(samples_here, side, side, inputs.shape[3]), jnp.stack(grad_taps, axis=1))


def one_layer(inputs, upstream, bank_part, coefs, side):
    flat_bank = bank_part.reshape(BANKS, -1).astype(jnp.float32)
    mixed_all = jnp.dot(coefs, flat_bank, precision=HIGH)
    mixed_all = mixed_all.reshape((coefs.shape[0],) + bank_part.shape[1:]).astype(jnp.bfloat16)
    kernels = lax.all_to_all(mixed_all, "batch", split_axis=0, concat_axis=2, tiled=True)
    delta, kernel_grad = local_grads(inputs, upstream, kernels, side)
    delta_total = lax.psum(delta.astype(jnp.bfloat16), "chan").astype(jnp.float32)
    width = delta.shape[3] // lax.axis_size("chan")
    delta_part = lax.dynamic_slice_in_dim(delta_total, lax.axis_index("chan") * width, width, 3)
    moved = lax.all_to_all(
        kernel_grad.astype(jnp.bfloat16), "batch", split_axis=2, concat_axis=0, tiled=True
    ).astype(kernel_grad.dtype)
    flat_grads = moved.reshape(moved.shape[0], -1)
    update = jnp.dot(coefs.T, flat_grads, precision=HIGH).reshape(bank_part.shape)
    dcoef_part = lax.dot_general(flat_grads, flat_bank, (((1,), (1,)), ((), ())), precision=HIGH)
    return (delta_part.astype(jnp.bfloat16), update, dcoef_part)


def logit_grads(coefs, totals, samples_here):
    first_row = lax.axis_index("batch") * samples_here
    own_coefs = lax.dynamic_slice_in_dim(coefs, first_row, samples_here, 0)
    own_totals = lax.dynamic_slice_in_dim(totals, first_row, samples_here, 0)
    return own_coefs * (own_totals - jnp.sum(own_coefs * own_totals, axis=1, keepdims=True))


def per_device(
    fine_inputs,
    fine_upstream,
    fine_bank,
    fine_coefs,
    coarse_inputs,
    coarse_upstream,
    coarse_bank,
    coarse_coefs,
):
    fine_delta, fine_update, fine_partial = one_layer(
        fine_inputs, fine_upstream, fine_bank, fine_coefs, FINE_SIDE
    )
    coarse_delta, coarse_update, coarse_partial = one_layer(
        coarse_inputs, coarse_upstream, coarse_bank, coarse_coefs, COARSE_SIDE
    )
    fine_total, coarse_total = lax.psum((fine_partial, coarse_partial), ("batch", "chan"))
    samples_here = fine_inputs.shape[0]
    fine_logit = logit_grads(fine_coefs, fine_total, samples_here)
    coarse_logit = logit_grads(coarse_coefs, coarse_total, samples_here)
    return (fine_delta, fine_update, fine_logit, coarse_delta, coarse_update, coarse_logit)


def solution(mesh):
    return jax.shard_map(
        per_device,
        mesh=mesh,
        in_specs=(
            P("batch", None, None, None),
            P("batch", None, None, "chan"),
            P(None, None, "batch", "chan"),
            P(),
            P("batch", None, None, None),
            P("batch", None, None, "chan"),
            P(None, None, "batch", "chan"),
            P(),
        ),
        out_specs=(
            P("batch", None, None, "chan"),
            P(None, None, "batch", "chan"),
            P("batch", None),
            P("batch", None, None, "chan"),
            P(None, None, "batch", "chan"),
            P("batch", None),
        ),
        check_vma=False,
    )
```

profile of v0, /device:TPU:10, one launch (start us, length us, event | category | flops | bytes accessed | tf_op | source)
XLA Modules:
  0.0 182.0 jit_solution(2190526697358805732)
XLA Ops:
  7.2 2.0 %copy.47 = bf16[1,8,576,128]{3,1,2,0:T(8,128)(2,1)S(1)} copy(bf16[1,8,576,128]{3,2,1,0:T(8,128)(2,1)} %bitcast.542) | data formatting | bytes 2359296
  9.2 1.1 convolution_convert_fusion.1
  10.3 1.3 copy.24
  11.6 4.4 %all-to-all-start = ((bf16[8,9,64,128]{3,2,1,0:T(8,128)(2,1)}), bf16[8,9,64,128]{3,2,1,0:T(8,128)(2,1)S(1)}, u32[]{:S(2)}, u32[]{:S(2)}) async-start(bf16[8,9,64,128]{3,2,1,0:T(8,128)(2,1)} %copy.24), calls=%async_computation | async-start | bytes 2359296 | tf_op jit(solution)/shard_map/all_to_all | solution.py:43
  16.0 0.8 copy.46
  24.5 1.1 convolution_convert_fusion
  25.9 1.3 copy.29
  27.2 2.2 %copy.27 = bf16[1,9,512,128]{3,1,0,2:T(8,128)(2,1)} copy(bf16[1,9,512,128]{3,2,1,0:T(8,128)(2,1)S(1)} %fusion.62) | data formatting | bytes 2359296 | tf_op jit(solution)/shard_map/stack | solution.py:36
  29.5 1.3 fusion.48
  31.4 2.2 %copy.31 = bf16[1,9,512,128]{3,1,0,2:T(8,128)(2,1)} copy(bf16[1,9,512,128]{3,2,1,0:T(8,128)(2,1)S(1)} %fusion.44) | data formatting | bytes 2359296 | tf_op jit(solution)/shard_map/stack | solution.py:36
  33.6 0.8 pad_slice_fusion.24
  34.4 1.2 pad_slice_fusion.16
  35.6 4.3 %all-to-all-start.1 = ((bf16[1,9,512,128]{3,1,0,2:T(8,128)(2,1)}), bf16[1,9,512,128]{3,1,0,2:T(8,128)(2,1)}, u32[]{:S(2)}, u32[]{:S(2)}) async-start(bf16[1,9,512,128]{3,1,0,2:T(8,128)(2,1)} %copy.27), calls=%async_computation.1 | async-start | bytes 4194304 | tf_op jit(solution)/shard_map/all_to_all | solution.py:48
  40.5 1.8 fusion.124
  42.2 1.7 fusion.125
  44.0 1.7 fusion.126
  45.7 19.4 %all-to-all-done.1 = bf16[1,9,512,128]{3,1,0,2:T(8,128)(2,1)} async-done(((bf16[1,9,512,128]{3,1,0,2:T(8,128)(2,1)}), bf16[1,9,512,128]{3,1,0,2:T(8,128)(2,1)}, u32[]{:S(2)}, u32[]{:S(2)}) %all-to-all-start.1) | async-done | bytes 1179680 | tf_op jit(solution)/shard_map/all_to_all | solution.py:48
  65.1 5.7 %all-to-all-start.2 = ((bf16[8,9,64,128]{3,2,1,0:T(8,128)(2,1)}), bf16[8,9,64,128]{3,2,1,0:T(8,128)(2,1)}, u32[]{:S(2)}, u32[]{:S(2)}) async-start(bf16[8,9,64,128]{3,2,1,0:T(8,128)(2,1)} %copy.29), calls=%async_computation.2 | async-start | bytes 2359296 | tf_op jit(solution)/shard_map/all_to_all | solution.py:43
  70.8 3.0 %copy.49 = bf16[1,9,8,64,128]{4,3,1,2,0:T(8,128)(2,1)} copy(bf16[1,9,8,64,128]{4,1,3,2,0:T(8,128)(2,1)} %bitcast.57) | data formatting | bytes 2359296 | tf_op jit(solution)/shard_map/all_to_all | solution.py:48
  73.8 1.8 reshape.837
  75.5 2.9 %fusion.127 = f32[1024,512]{1,0:T(8,128)} fusion(bf16[1024,128]{1,0:T(8,128)(2,1)} %bitcast.554, bf16[1,9,512,128]{3,2,1,0:T(8,128)(2,1)} %bitcast.526), kind=kOutput, calls=%fused_computation.192 | convolution fusion | flops 134217728 | bytes 2490368 | tf_op jit(solution)/shard_map/bpo,bco->bpc/dot_general | solution.py:33
  78.4 2.7 %fusion.128 = f32[1024,512]{1,0:T(8,128)} fusion(bf16[1024,128]{1,0:T(8,128)(2,1)S(1)} %bitcast.553, bf16[1,9,512,128]{3,2,1,0:T(8,128)(2,1)} %bitcast.527), kind=kOutput, calls=%fused_computation.194 | convolution fusion | flops 134217728 | bytes 2490368 | tf_op jit(solution)/shard_map/bpo,bco->bpc/dot_general | solution.py:33
  81.1 2.7 %fusion.130 = f32[1024,512]{1,0:T(8,128)} fusion(bf16[1024,128]{1,0:T(8,128)(2,1)S(1)} %bitcast.552, bf16[1,9,512,128]{3,2,1,0:T(8,128)(2,1)} %bitcast.528), kind=kOutput, calls=%fused_computation.198 | convolution fusion | flops 134217728 | bytes 2490368 | tf_op jit(solution)/shard_map/bpo,bco->bpc/dot_general | solution.py:33
  83.8 2.7 %fusion.129 = f32[1024,512]{1,0:T(8,128)} fusion(bf16[1024,128]{1,0:T(8,128)(2,1)S(1)} %bitcast.551, bf16[1,9,512,128]{3,2,1,0:T(8,128)(2,1)} %bitcast.529), kind=kOutput, calls=%fused_computation.196 | convolution fusion | flops 134217728 | bytes 2490368 | tf_op jit(solution)/shard_map/bpo,bco->bpc/dot_general | solution.py:33
  86.5 5.4 %all-to-all-start.3 = ((bf16[1,9,512,128]{3,1,0,2:T(8,128)(2,1)}), bf16[1,9,512,128]{3,1,0,2:T(8,128)(2,1)}, u32[]{:S(2)}, u32[]{:S(2)}) async-start(bf16[1,9,512,128]{3,1,0,2:T(8,128)(2,1)} %copy.31), calls=%async_computation.3 | async-start | bytes 4194304 | tf_op jit(solution)/shard_map/all_to_all | solution.py:48
  91.9 1.5 copy.30
  93.5 1.1 fusion.122
  94.6 1.1 convolution_add_fusion.6
  95.8 1.2 convolution_add_fusion.5
  97.0 1.2 convolution_add_fusion.4
  98.5 1.2 convolution_add_fusion.3
  100.2 1.9 %fusion.6 = bf16[256,512]{1,0:T(8,128)(2,1)} fusion(f32[256,512]{1,0:T(8,128)S(1)} %convolution_add_fusion.1, bf16[256,128]{1,0:T(8,128)(2,1)} %bitcast.567, bf16[1,9,512,128]{3,2,1,0:T(8,128)(2,1)S(1)} %bitcast.539), kind=kOutput, calls=%fused_computation.25 | convolution fusion | flops 33816576 | bytes 983040 | tf_op jit(solution)/shard_map/bpo,bco->bpc/dot_general | solution.py:33
  102.2 3.8 %fusion.4 = bf16[1024,512]{1,0:T(8,128)(2,1)} fusion(f32[1024,512]{1,0:T(8,128)S(1)} %fusion.123, f32[1024,512]{1,0:T(8,128)S(1)} %copy-done, f32[1024,512]{1,0:T(8,128)S(1)} %copy-done.1, f32[512,1024]{0,1:T(8,128)S(1)} %copy-done.2, f32[1024,512]{1,0:T(8,128)S(1)} %copy-done.3, f32[1024,512]{1,0:T(8,128)S(1)} %copy-done.4, f32[1024,512]{1,0:T(8,128)S(1)} %copy-done.5, ...), kind=kOutput, calls=%fused_computation.5 | convolution fusion | flops 138936320 | bytes 18219008 | tf_op jit(solution)/shard_map/bpo,bco->bpc/dot_general | solution.py:33
  106.0 1.2 fusion.160
  107.2 1.8 %copy.33 = f32[8,9,64,128]{3,2,1,0:T(8,128)} copy(f32[8,9,64,128]{3,0,2,1:T(8,128)S(1)} %bitcast.520) | data formatting | bytes 4718592
  109.0 8.1 %all-to-all-done.3 = bf16[1,9,512,128]{3,1,0,2:T(8,128)(2,1)} async-done(((bf16[1,9,512,128]{3,1,0,2:T(8,128)(2,1)}), bf16[1,9,512,128]{3,1,0,2:T(8,128)(2,1)}, u32[]{:S(2)}, u32[]{:S(2)}) %all-to-all-start.3) | async-done | bytes 1179680 | tf_op jit(solution)/shard_map/all_to_all | solution.py:48
  117.2 1.9 %copy.48 = bf16[1,9,8,64,128]{4,3,1,2,0:T(8,128)(2,1)S(1)} copy(bf16[1,9,8,64,128]{4,1,3,2,0:T(8,128)(2,1)} %bitcast.118) | data formatting | bytes 2359296 | tf_op jit(solution)/shard_map/all_to_all | solution.py:48
  119.6 1.2 fusion.161
  120.8 1.8 %copy.34 = f32[8,9,64,128]{3,2,1,0:T(8,128)} copy(f32[8,9,64,128]{3,0,2,1:T(8,128)S(1)} %bitcast.521) | data formatting | bytes 4718592
  122.6 1.1 fusion.158
  123.9 1.1 fusion.159
  125.0 43.5 %all-reduce.4 = (f32[8,8]{1,0:T(8,128)S(1)}, f32[8,8]{1,0:T(8,128)S(1)}) all-reduce(f32[8,8]{1,0:T(8,128)S(1)} %fusion.158, f32[8,8]{1,0:T(8,128)S(1)} %fusion.159), channel_id=1, replica_groups=mesh['batch'=8,'chan'=4] {'batch','chan'}, use_global_device_ids=true, to_apply=%region_1.2 | all-reduce | flops 128 | bytes 1024 | tf_op jit(solution)/shard_map/psum | solution.py:80
  168.4 0.6 multiply_reduce_fusion.1
  169.0 0.6 multiply_reduce_fusion
  169.6 1.2 subtract_multiply_fusion.1
  170.8 1.2 subtract_multiply_fusion
  172.0 1.7 convert_convert_fusion
  173.6 1.5 convert_convert_fusion.1
  (78 shorter events, 10.6 us)
Async XLA Ops:
  7.2 2.1 %copy-start.20 = (f32[8,8]{1,0:T(8,128)S(1)}, f32[8,8]{1,0:T(8,128)}, u32[]{:S(2)}) copy-start(f32[8,8]{1,0:T(8,128)} %param.11) | copy-start | bytes 772
  11.6 4.4 %copy-start.8 = (bf16[8,9,64,128]{3,2,1,0:T(8,128)(2,1)S(1)}, bf16[8,9,64,128]{3,2,1,0:T(8,128)(2,1)}, u32[]{:S(2)}) copy-start(bf16[8,9,64,128]{3,2,1,0:T(8,128)(2,1)} %param.14) | copy-start | bytes 3538948
  11.6 24.0 %all-to-all-start = ((bf16[8,9,64,128]{3,2,1,0:T(8,128)(2,1)}), bf16[8,9,64,128]{3,2,1,0:T(8,128)(2,1)S(1)}, u32[]{:S(2)}, u32[]{:S(2)}) async-start(bf16[8,9,64,128]{3,2,1,0:T(8,128)(2,1)} %copy.24), calls=%async_computation | async-start | bytes 2359296 | tf_op jit(solution)/shard_map/all_to_all | solution.py:43
  16.0 1.0 copy-start.10
  16.0 1.3 copy-start.22
  21.7 0.8 copy-start.15
  21.7 1.0 copy-start.23
  23.9 0.7 copy-start.21
  29.5 1.3 copy-start.16
  29.5 1.3 copy-start.24
  31.4 3.0 %copy-start.11 = (bf16[1,32,32,128]{3,2,1,0:T(8,128)(2,1)S(1)}, bf16[1,32,32,128]{3,2,1,0:T(8,128)(2,1)}, u32[]{:S(2)}) copy-start(bf16[1,32,32,128]{3,2,1,0:T(8,128)(2,1)} %param.9) | copy-start | bytes 786436
  35.6 29.5 %all-to-all-start.1 = ((bf16[1,9,512,128]{3,1,0,2:T(8,128)(2,1)}), bf16[1,9,512,128]{3,1,0,2:T(8,128)(2,1)}, u32[]{:S(2)}, u32[]{:S(2)}) async-start(bf16[1,9,512,128]{3,1,0,2:T(8,128)(2,1)} %copy.27), calls=%async_computation.1 | async-start | bytes 4194304 | tf_op jit(solution)/shard_map/all_to_all | solution.py:48
  40.0 4.0 %copy-start.6 = (bf16[8,9,64,128]{3,2,0,1:T(8,128)(2,1)}, bf16[8,9,64,128]{3,2,0,1:T(8,128)(2,1)S(1)}, u32[]{:S(2)}) copy-start(bf16[8,9,64,128]{3,2,0,1:T(8,128)(2,1)S(1)} %copy.25) | copy-start | bytes 3538948
  65.1 21.4 %all-to-all-start.2 = ((bf16[8,9,64,128]{3,2,1,0:T(8,128)(2,1)}), bf16[8,9,64,128]{3,2,1,0:T(8,128)(2,1)}, u32[]{:S(2)}, u32[]{:S(2)}) async-start(bf16[8,9,64,128]{3,2,1,0:T(8,128)(2,1)} %copy.29), calls=%async_computation.2 | async-start | bytes 2359296 | tf_op jit(solution)/shard_map/all_to_all | solution.py:43
  75.5 2.9 %copy-start.14 = (bf16[1,32,32,128]{3,2,1,0:T(8,128)(2,1)S(1)}, bf16[1,32,32,128]{3,2,1,0:T(8,128)(2,1)}, u32[]{:S(2)}) copy-start(bf16[1,32,32,128]{3,2,1,0:T(8,128)(2,1)} %get-tuple-element.30) | copy-start | bytes 786436
  78.4 2.7 %copy-start.13 = (bf16[1,32,32,128]{3,2,1,0:T(8,128)(2,1)S(1)}, bf16[1,32,32,128]{3,2,1,0:T(8,128)(2,1)}, u32[]{:S(2)}) copy-start(bf16[1,32,32,128]{3,2,1,0:T(8,128)(2,1)} %get-tuple-element.35) | copy-start | bytes 786436
  81.1 2.7 %copy-start.12 = (bf16[1,32,32,128]{3,2,1,0:T(8,128)(2,1)S(1)}, bf16[1,32,32,128]{3,2,1,0:T(8,128)(2,1)}, u32[]{:S(2)}) copy-start(bf16[1,32,32,128]{3,2,1,0:T(8,128)(2,1)} %get-tuple-element.29) | copy-start | bytes 786436
  86.5 30.6 %all-to-all-start.3 = ((bf16[1,9,512,128]{3,1,0,2:T(8,128)(2,1)}), bf16[1,9,512,128]{3,1,0,2:T(8,128)(2,1)}, u32[]{:S(2)}, u32[]{:S(2)}) async-start(bf16[1,9,512,128]{3,1,0,2:T(8,128)(2,1)} %copy.31), calls=%async_computation.3 | async-start | bytes 4194304 | tf_op jit(solution)/shard_map/all_to_all | solution.py:48
  91.9 80.0 %all-reduce.8.cloned.1.call-start = ((), (), s32[]{:S(2)}) async-start(), calls=%async_computation.4 | async-start | bytes 2621440 | tf_op jit(solution)/shard_map/psum | solution.py:45
  91.9 10.2 %copy-start.4 = (f32[1024,512]{1,0:T(8,128)S(1)}, f32[1024,512]{1,0:T(8,128)}, u32[]{:S(2)}) copy-start(f32[1024,512]{1,0:T(8,128)} %fusion.128) | copy-start | bytes 6291460
  91.9 10.2 %copy-start.5 = (f32[1024,512]{1,0:T(8,128)S(1)}, f32[1024,512]{1,0:T(8,128)}, u32[]{:S(2)}) copy-start(f32[1024,512]{1,0:T(8,128)} %fusion.130) | copy-start | bytes 6291460
  94.6 5.1 %copy-start.19 = (bf16[1,16,16,128]{3,2,1,0:T(8,128)(2,1)S(1)}, bf16[1,16,16,128]{3,2,1,0:T(8,128)(2,1)}, u32[]{:S(2)}) copy-start(bf16[1,16,16,128]{3,2,1,0:T(8,128)(2,1)} %get-tuple-element.41) | copy-start | bytes 196612
  94.6 5.4 %copy-start.18 = (bf16[1,16,16,128]{3,2,1,0:T(8,128)(2,1)S(1)}, bf16[1,16,16,128]{3,2,1,0:T(8,128)(2,1)}, u32[]{:S(2)}) copy-start(bf16[1,16,16,128]{3,2,1,0:T(8,128)(2,1)} %get-tuple-element.42) | copy-start | bytes 196612
  95.7 2.5 %copy-start.17 = (bf16[1,16,16,128]{3,2,1,0:T(8,128)(2,1)S(1)}, bf16[1,16,16,128]{3,2,1,0:T(8,128)(2,1)}, u32[]{:S(2)}) copy-start(bf16[1,16,16,128]{3,2,1,0:T(8,128)(2,1)} %param.13) | copy-start | bytes 196612
  95.8 6.4 %copy-start.3 = (f32[1024,512]{1,0:T(8,128)S(1)}, f32[1024,512]{1,0:T(8,128)}, u32[]{:S(2)}) copy-start(f32[1024,512]{1,0:T(8,128)} %fusion.127) | copy-start | bytes 6291460
  97.0 5.2 %copy-start.2 = (f32[512,1024]{0,1:T(8,128)S(1)}, f32[512,1024]{0,1:T(8,128)}, u32[]{:S(2)}) copy-start(f32[512,1024]{0,1:T(8,128)} %fusion.126) | copy-start | bytes 6291460
  98.5 3.7 %copy-start.1 = (f32[1024,512]{1,0:T(8,128)S(1)}, f32[1024,512]{1,0:T(8,128)}, u32[]{:S(2)}) copy-start(f32[1024,512]{1,0:T(8,128)} %fusion.125) | copy-start | bytes 6291460
  100.0 2.2 %copy-start = (f32[1024,512]{1,0:T(8,128)S(1)}, f32[1024,512]{1,0:T(8,128)}, u32[]{:S(2)}) copy-start(f32[1024,512]{1,0:T(8,128)} %fusion.124) | copy-start | bytes 6291460
  120.8 1.8 %copy-start.7 = (bf16[8,9,64,128]{3,2,1,0:T(8,128)(2,1)S(1)}, bf16[8,9,64,128]{3,2,1,0:T(8,128)(2,1)}, u32[]{:S(2)}) copy-start(bf16[8,9,64,128]{3,2,1,0:T(8,128)(2,1)} %param.10) | copy-start | bytes 3538948
  122.6 1.3 copy-start.9
Sparse Core Ops, SparseCore 0:
  106.1 61.7 all-reduce.7
where the time goes:
time: 183 us; the launch traced here: 182 us
  matrix products  44.1 us (24%)
  blocking collectives  43.5 us (24%)
  waiting for transfers between devices  27.5 us (15%)
  local copies, waits for them, and re-layouts  26 us (14%)
  starting transfers between devices  19.8 us (11%)
  between operations  14.5 us (8%)
  other arithmetic  6.68 us (4%)
    psum x1, blocking collectives, per_device(): lax.psum((fine_partial, coarse_partial), ('batch', 'chan'))  43.5 us
    dot_general x18, matrix products, local_grads(): jnp.einsum('bpo,bco->bpc', window_up, kernels[:, tap], preferred_element_...  29 us
    all_to_all x2, waiting for transfers between devices, one_layer(): lax.all_to_all(kernel_grad.astype(jnp.bfloat16), 'batch', split_axis=2, c...  27.5 us
    all_to_all x2, starting transfers between devices, one_layer(): lax.all_to_all(mixed_all, 'batch', split_axis=0, concat_axis=2, tiled=True)  10 us
    all_to_all x2, starting transfers between devices, one_layer(): lax.all_to_all(kernel_grad.astype(jnp.bfloat16), 'batch', split_axis=2, c...  9.71 us
    dot_general x18, matrix products, local_grads(): jnp.einsum('bpc,bpo->bco', window_in, flat_up, preferred_element_type=jnp...  8.47 us
    unnamed x54, local copies, waits for them, and re-layouts  8.13 us
    all_to_all x2, local copies, waits for them, and re-layouts, one_layer(): lax.all_to_all(kernel_grad.astype(jnp.bfloat16), 'batch', split_axis=2, c...  4.92 us
  transfers between devices with their start and end apart: 5, of which 2 were waited for; matrix products, arithmetic and copies ran while one was open for 37% of the time, Pallas kernels for 0%

commit v1 on v0

--- a/solution.py
+++ b/solution.py
@@ -77,7 +77,9 @@
     coarse_delta, coarse_update, coarse_partial = one_layer(
         coarse_inputs, coarse_upstream, coarse_bank, coarse_coefs, COARSE_SIDE
     )
-    fine_total, coarse_total = lax.psum((fine_partial, coarse_partial), ("batch", "chan"))
+    fine_total, coarse_total = lax.psum(
+        lax.psum((fine_partial, coarse_partial), axis_name="chan"), axis_name="batch"
+    )
     samples_here = fine_inputs.shape[0]
     fine_logit = logit_grads(fine_coefs, fine_total, samples_here)
     coarse_logit = logit_grads(coarse_coefs, coarse_total, samples_here)

time: 183 us -> 181 us (0.989); the launches traced: 182 us -> 178 us
  blocking collectives: 43.5 us -> 20 us
  waiting for transfers between devices: 27.5 us -> 46.9 us
    psum x1 -> x2, blocking collectives: 43.5 us -> 20 us  [the longest x1 10.3 us: per_device(): lax.psum(lax.psum((fine_partial, coarse_partial), axis_name='chan'), axis...]
    psum x1, waiting for transfers between devices: 0.01 us -> 19.4 us  [one_layer(): lax.psum(delta.astype(jnp.bfloat16), 'chan').astype(jnp.float32)]
  transfers between devices with their start and end apart: 5 -> 5, of which waited for: 2 -> 3; matrix products, arithmetic and copies ran while one was open for 37% -> 38% of each run, Pallas kernels for 0% -> 0%
where the time goes in v1:
time: 181 us; the launch traced here: 178 us
  waiting for transfers between devices  46.9 us (26%)
  matrix products  44.1 us (24%)
  local copies, waits for them, and re-layouts  26 us (14%)
  blocking collectives  20 us (11%)
  starting transfers between devices  19.7 us (11%)
  between operations  14.5 us (8%)
  other arithmetic  6.68 us (4%)
    dot_general x18, matrix products, local_grads(): jnp.einsum('bpo,bco->bpc', window_up, kernels[:, tap], preferred_element_...  29 us
    all_to_all x2, waiting for transfers between devices, one_layer(): lax.all_to_all(kernel_grad.astype(jnp.bfloat16), 'batch', split_axis=2, c...  27.5 us
    psum x1, waiting for transfers between devices, one_layer(): lax.psum(delta.astype(jnp.bfloat16), 'chan').astype(jnp.float32)  19.4 us
    psum x1, blocking collectives, per_device(): lax.psum(lax.psum((fine_partial, coarse_partial), axis_name='chan'), axis...  10.3 us
    all_to_all x2, starting transfers between devices, one_layer(): lax.all_to_all(mixed_all, 'batch', split_axis=0, concat_axis=2, tiled=True)  10 us
    all_to_all x2, starting transfers between devices, one_layer(): lax.all_to_all(kernel_grad.astype(jnp.bfloat16), 'batch', split_axis=2, c...  9.7 us
    psum x1, blocking collectives, per_device(): lax.psum((fine_partial, coarse_partial), axis_name='chan')  9.69 us
    dot_general x18, matrix products, local_grads(): jnp.einsum('bpc,bpo->bco', window_in, flat_up, preferred_element_type=jnp...  8.47 us
  transfers between devices with their start and end apart: 5, of which 3 were waited for; matrix products, arithmetic and copies ran while one was open for 38% of the time, Pallas kernels for 0%

profile of v1, /device:TPU:10, one launch (start us, length us, event | category | flops | bytes accessed | tf_op | source)
XLA Modules:
  0.0 177.9 jit_solution(14856702704978234312)
XLA Ops:
  7.2 2.0 %copy.47 = bf16[1,8,576,128]{3,1,2,0:T(8,128)(2,1)S(1)} copy(bf16[1,8,576,128]{3,2,1,0:T(8,128)(2,1)} %bitcast.542) | data formatting | bytes 2359296
  9.2 1.1 convolution_convert_fusion.1
  10.3 1.3 copy.24
  11.6 4.4 %all-to-all-start = ((bf16[8,9,64,128]{3,2,1,0:T(8,128)(2,1)}), bf16[8,9,64,128]{3,2,1,0:T(8,128)(2,1)S(1)}, u32[]{:S(2)}, u32[]{:S(2)}) async-start(bf16[8,9,64,128]{3,2,1,0:T(8,128)(2,1)} %copy.24), calls=%async_computation | async-start | bytes 2359296 | tf_op jit(solution)/shard_map/all_to_all | solution.py:43
  16.0 0.8 copy.46
  24.5 1.1 convolution_convert_fusion
  25.9 1.3 copy.29
  27.3 2.2 %copy.27 = bf16[1,9,512,128]{3,1,0,2:T(8,128)(2,1)} copy(bf16[1,9,512,128]{3,2,1,0:T(8,128)(2,1)S(1)} %fusion.62) | data formatting | bytes 2359296 | tf_op jit(solution)/shard_map/stack | solution.py:36
  29.5 1.3 fusion.48
  31.4 2.2 %copy.31 = bf16[1,9,512,128]{3,1,0,2:T(8,128)(2,1)} copy(bf16[1,9,512,128]{3,2,1,0:T(8,128)(2,1)S(1)} %fusion.44) | data formatting | bytes 2359296 | tf_op jit(solution)/shard_map/stack | solution.py:36
  33.6 0.8 pad_slice_fusion.24
  34.4 1.2 pad_slice_fusion.16
  35.6 4.3 %all-to-all-start.1 = ((bf16[1,9,512,128]{3,1,0,2:T(8,128)(2,1)}), bf16[1,9,512,128]{3,1,0,2:T(8,128)(2,1)}, u32[]{:S(2)}, u32[]{:S(2)}) async-start(bf16[1,9,512,128]{3,1,0,2:T(8,128)(2,1)} %copy.27), calls=%async_computation.1 | async-start | bytes 4194304 | tf_op jit(solution)/shard_map/all_to_all | solution.py:48
  40.5 1.8 fusion.124
  42.2 1.7 fusion.125
  44.0 1.7 fusion.126
  45.7 19.4 %all-to-all-done.1 = bf16[1,9,512,128]{3,1,0,2:T(8,128)(2,1)} async-done(((bf16[1,9,512,128]{3,1,0,2:T(8,128)(2,1)}), bf16[1,9,512,128]{3,1,0,2:T(8,128)(2,1)}, u32[]{:S(2)}, u32[]{:S(2)}) %all-to-all-start.1) | async-done | bytes 1179680 | tf_op jit(solution)/shard_map/all_to_all | solution.py:48
  65.1 5.7 %all-to-all-start.2 = ((bf16[8,9,64,128]{3,2,1,0:T(8,128)(2,1)}), bf16[8,9,64,128]{3,2,1,0:T(8,128)(2,1)}, u32[]{:S(2)}, u32[]{:S(2)}) async-start(bf16[8,9,64,128]{3,2,1,0:T(8,128)(2,1)} %copy.29), calls=%async_computation.2 | async-start | bytes 2359296 | tf_op jit(solution)/shard_map/all_to_all | solution.py:43
  70.8 3.0 %copy.49 = bf16[1,9,8,64,128]{4,3,1,2,0:T(8,128)(2,1)} copy(bf16[1,9,8,64,128]{4,1,3,2,0:T(8,128)(2,1)} %bitcast.57) | data formatting | bytes 2359296 | tf_op jit(solution)/shard_map/all_to_all | solution.py:48
  73.8 1.8 reshape.837
  75.5 2.9 %fusion.127 = f32[1024,512]{1,0:T(8,128)} fusion(bf16[1024,128]{1,0:T(8,128)(2,1)} %bitcast.554, bf16[1,9,512,128]{3,2,1,0:T(8,128)(2,1)} %bitcast.526), kind=kOutput, calls=%fused_computation.192 | convolution fusion | flops 134217728 | bytes 2490368 | tf_op jit(solution)/shard_map/bpo,bco->bpc/dot_general | solution.py:33
  78.4 2.7 %fusion.128 = f32[1024,512]{1,0:T(8,128)} fusion(bf16[1024,128]{1,0:T(8,128)(2,1)S(1)} %bitcast.553, bf16[1,9,512,128]{3,2,1,0:T(8,128)(2,1)} %bitcast.527), kind=kOutput, calls=%fused_computation.194 | convolution fusion | flops 134217728 | bytes 2490368 | tf_op jit(solution)/shard_map/bpo,bco->bpc/dot_general | solution.py:33
  81.1 2.7 %fusion.130 = f32[1024,512]{1,0:T(8,128)} fusion(bf16[1024,128]{1,0:T(8,128)(2,1)S(1)} %bitcast.552, bf16[1,9,512,128]{3,2,1,0:T(8,128)(2,1)} %bitcast.528), kind=kOutput, calls=%fused_computation.198 | convolution fusion | flops 134217728 | bytes 2490368 | tf_op jit(solution)/shard_map/bpo,bco->bpc/dot_general | solution.py:33
  83.8 2.7 %fusion.129 = f32[1024,512]{1,0:T(8,128)} fusion(bf16[1024,128]{1,0:T(8,128)(2,1)S(1)} %bitcast.551, bf16[1,9,512,128]{3,2,1,0:T(8,128)(2,1)} %bitcast.529), kind=kOutput, calls=%fused_computation.196 | convolution fusion | flops 134217728 | bytes 2490368 | tf_op jit(solution)/shard_map/bpo,bco->bpc/dot_general | solution.py:33
  86.5 5.4 %all-to-all-start.3 = ((bf16[1,9,512,128]{3,1,0,2:T(8,128)(2,1)}), bf16[1,9,512,128]{3,1,0,2:T(8,128)(2,1)}, u32[]{:S(2)}, u32[]{:S(2)}) async-start(bf16[1,9,512,128]{3,1,0,2:T(8,128)(2,1)} %copy.31), calls=%async_computation.3 | async-start | bytes 4194304 | tf_op jit(solution)/shard_map/all_to_all | solution.py:48
  91.9 1.5 copy.30
  93.5 1.1 fusion.122
  94.6 1.1 convolution_add_fusion.6
  95.8 1.2 convolution_add_fusion.5
  97.0 1.2 convolution_add_fusion.4
  98.5 1.2 convolution_add_fusion.3
  100.2 1.9 %fusion.6 = bf16[256,512]{1,0:T(8,128)(2,1)} fusion(f32[256,512]{1,0:T(8,128)S(1)} %convolution_add_fusion.1, bf16[256,128]{1,0:T(8,128)(2,1)} %bitcast.567, bf16[1,9,512,128]{3,2,1,0:T(8,128)(2,1)S(1)} %bitcast.539), kind=kOutput, calls=%fused_computation.25 | convolution fusion | flops 33816576 | bytes 983040 | tf_op jit(solution)/shard_map/bpo,bco->bpc/dot_general | solution.py:33
  102.2 3.8 %fusion.4 = bf16[1024,512]{1,0:T(8,128)(2,1)} fusion(f32[1024,512]{1,0:T(8,128)S(1)} %fusion.123, f32[1024,512]{1,0:T(8,128)S(1)} %copy-done, f32[1024,512]{1,0:T(8,128)S(1)} %copy-done.1, f32[512,1024]{0,1:T(8,128)S(1)} %copy-done.2, f32[1024,512]{1,0:T(8,128)S(1)} %copy-done.3, f32[1024,512]{1,0:T(8,128)S(1)} %copy-done.4, f32[1024,512]{1,0:T(8,128)S(1)} %copy-done.5, ...), kind=kOutput, calls=%fused_computation.5 | convolution fusion | flops 138936320 | bytes 18219008 | tf_op jit(solution)/shard_map/bpo,bco->bpc/dot_general | solution.py:33
  106.0 1.2 fusion.160
  107.2 1.8 %copy.33 = f32[8,9,64,128]{3,2,1,0:T(8,128)} copy(f32[8,9,64,128]{3,0,2,1:T(8,128)S(1)} %bitcast.520) | data formatting | bytes 4718592
  109.0 8.1 %all-to-all-done.3 = bf16[1,9,512,128]{3,1,0,2:T(8,128)(2,1)} async-done(((bf16[1,9,512,128]{3,1,0,2:T(8,128)(2,1)}), bf16[1,9,512,128]{3,1,0,2:T(8,128)(2,1)}, u32[]{:S(2)}, u32[]{:S(2)}) %all-to-all-start.3) | async-done | bytes 1179680 | tf_op jit(solution)/shard_map/all_to_all | solution.py:48
  117.2 1.9 %copy.48 = bf16[1,9,8,64,128]{4,3,1,2,0:T(8,128)(2,1)S(1)} copy(bf16[1,9,8,64,128]{4,1,3,2,0:T(8,128)(2,1)} %bitcast.118) | data formatting | bytes 2359296 | tf_op jit(solution)/shard_map/all_to_all | solution.py:48
  119.6 1.2 fusion.161
  120.8 1.8 %copy.34 = f32[8,9,64,128]{3,2,1,0:T(8,128)} copy(f32[8,9,64,128]{3,0,2,1:T(8,128)S(1)} %bitcast.521) | data formatting | bytes 4718592
  122.6 1.1 fusion.158
  123.9 1.1 fusion.159
  125.0 9.7 %all-reduce.5 = (f32[8,8]{1,0:T(8,128)S(1)}, f32[8,8]{1,0:T(8,128)S(1)}) all-reduce(f32[8,8]{1,0:T(8,128)S(1)} %fusion.158, f32[8,8]{1,0:T(8,128)S(1)} %fusion.159), channel_id=1, replica_groups=mesh['batch'=8,'chan'=4] {'chan'}, use_global_device_ids=true, to_apply=%region_1.2 | all-reduce | flops 128 | bytes 1024 | tf_op jit(solution)/shard_map/psum | solution.py:81
  134.7 10.3 %all-reduce.4 = (f32[8,8]{1,0:T(8,128)S(1)}, f32[8,8]{1,0:T(8,128)S(1)}) all-reduce(f32[8,8]{1,0:T(8,128)S(1)} %get-tuple-element.26, f32[8,8]{1,0:T(8,128)S(1)} %get-tuple-element.27), channel_id=1, replica_groups=mesh['batch'=8,'chan'=4] {'batch'}, use_global_device_ids=true, to_apply=%region_2.3 | all-reduce | flops 128 | bytes 1024 | tf_op jit(solution)/shard_map/psum | solution.py:80
  146.2 1.2 subtract_multiply_fusion.1
  147.3 1.2 subtract_multiply_fusion
  148.5 19.4 %all-reduce.9.cloned.1.call-done = (bf16[1,32,32,512]{3,2,1,0:T(8,128)(2,1)}, bf16[1,16,16,512]{3,2,1,0:T(8,128)(2,1)}) async-done(((bf16[1,32,32,512]{3,2,1,0:T(8,128)(2,1)}, bf16[1,16,16,512]{3,2,1,0:T(8,128)(2,1)}), (bf16[1,32,32,512]{3,2,1,0:T(8,128)(2,1)}, bf16[1,16,16,512]{3,2,1,0:T(8,128)(2,1)})) %all-reduce.9.cloned.1.call-update) | async-done | bytes 1310736 | tf_op jit(solution)/shard_map/psum | solution.py:45
  167.9 1.7 convert_convert_fusion
  169.6 1.5 convert_convert_fusion.1
  (79 shorter events, 11.8 us)
Async XLA Ops:
  7.2 2.1 %copy-start.20 = (f32[8,8]{1,0:T(8,128)S(1)}, f32[8,8]{1,0:T(8,128)}, u32[]{:S(2)}) copy-start(f32[8,8]{1,0:T(8,128)} %param.11) | copy-start | bytes 772
  11.6 4.4 %copy-start.8 = (bf16[8,9,64,128]{3,2,1,0:T(8,128)(2,1)S(1)}, bf16[8,9,64,128]{3,2,1,0:T(8,128)(2,1)}, u32[]{:S(2)}) copy-start(bf16[8,9,64,128]{3,2,1,0:T(8,128)(2,1)} %param.14) | copy-start | bytes 3538948
  11.6 24.0 %all-to-all-start = ((bf16[8,9,64,128]{3,2,1,0:T(8,128)(2,1)}), bf16[8,9,64,128]{3,2,1,0:T(8,128)(2,1)S(1)}, u32[]{:S(2)}, u32[]{:S(2)}) async-start(bf16[8,9,64,128]{3,2,1,0:T(8,128)(2,1)} %copy.24), calls=%async_computation | async-start | bytes 2359296 | tf_op jit(solution)/shard_map/all_to_all | solution.py:43
  16.0 1.0 copy-start.10
  16.0 1.3 copy-start.22
  21.7 0.8 copy-start.15
  21.7 1.0 copy-start.23
  23.9 0.7 copy-start.21
  29.5 1.3 copy-start.16
  29.5 1.3 copy-start.24
  31.4 3.0 %copy-start.11 = (bf16[1,32,32,128]{3,2,1,0:T(8,128)(2,1)S(1)}, bf16[1,32,32,128]{3,2,1,0:T(8,128)(2,1)}, u32[]{:S(2)}) copy-start(bf16[1,32,32,128]{3,2,1,0:T(8,128)(2,1)} %param.9) | copy-start | bytes 786436
  35.6 29.5 %all-to-all-start.1 = ((bf16[1,9,512,128]{3,1,0,2:T(8,128)(2,1)}), bf16[1,9,512,128]{3,1,0,2:T(8,128)(2,1)}, u32[]{:S(2)}, u32[]{:S(2)}) async-start(bf16[1,9,512,128]{3,1,0,2:T(8,128)(2,1)} %copy.27), calls=%async_computation.1 | async-start | bytes 4194304 | tf_op jit(solution)/shard_map/all_to_all | solution.py:48
  40.0 4.0 %copy-start.6 = (bf16[8,9,64,128]{3,2,0,1:T(8,128)(2,1)}, bf16[8,9,64,128]{3,2,0,1:T(8,128)(2,1)S(1)}, u32[]{:S(2)}) copy-start(bf16[8,9,64,128]{3,2,0,1:T(8,128)(2,1)S(1)} %copy.25) | copy-start | bytes 3538948
  65.1 21.4 %all-to-all-start.2 = ((bf16[8,9,64,128]{3,2,1,0:T(8,128)(2,1)}), bf16[8,9,64,128]{3,2,1,0:T(8,128)(2,1)}, u32[]{:S(2)}, u32[]{:S(2)}) async-start(bf16[8,9,64,128]{3,2,1,0:T(8,128)(2,1)} %copy.29), calls=%async_computation.2 | async-start | bytes 2359296 | tf_op jit(solution)/shard_map/all_to_all | solution.py:43
  75.5 2.9 %copy-start.14 = (bf16[1,32,32,128]{3,2,1,0:T(8,128)(2,1)S(1)}, bf16[1,32,32,128]{3,2,1,0:T(8,128)(2,1)}, u32[]{:S(2)}) copy-start(bf16[1,32,32,128]{3,2,1,0:T(8,128)(2,1)} %get-tuple-element.32) | copy-start | bytes 786436
  78.4 2.7 %copy-start.13 = (bf16[1,32,32,128]{3,2,1,0:T(8,128)(2,1)S(1)}, bf16[1,32,32,128]{3,2,1,0:T(8,128)(2,1)}, u32[]{:S(2)}) copy-start(bf16[1,32,32,128]{3,2,1,0:T(8,128)(2,1)} %get-tuple-element.37) | copy-start | bytes 786436
  81.1 2.7 %copy-start.12 = (bf16[1,32,32,128]{3,2,1,0:T(8,128)(2,1)S(1)}, bf16[1,32,32,128]{3,2,1,0:T(8,128)(2,1)}, u32[]{:S(2)}) copy-start(bf16[1,32,32,128]{3,2,1,0:T(8,128)(2,1)} %get-tuple-element.31) | copy-start | bytes 786436
  86.5 30.6 %all-to-all-start.3 = ((bf16[1,9,512,128]{3,1,0,2:T(8,128)(2,1)}), bf16[1,9,512,128]{3,1,0,2:T(8,128)(2,1)}, u32[]{:S(2)}, u32[]{:S(2)}) async-start(bf16[1,9,512,128]{3,1,0,2:T(8,128)(2,1)} %copy.31), calls=%async_computation.3 | async-start | bytes 4194304 | tf_op jit(solution)/shard_map/all_to_all | solution.py:48
  91.9 76.0 %all-reduce.9.cloned.1.call-start = ((), (), s32[]{:S(2)}) async-start(), calls=%async_computation.4 | async-start | bytes 2621440 | tf_op jit(solution)/shard_map/psum | solution.py:45
  91.9 10.2 %copy-start.4 = (f32[1024,512]{1,0:T(8,128)S(1)}, f32[1024,512]{1,0:T(8,128)}, u32[]{:S(2)}) copy-start(f32[1024,512]{1,0:T(8,128)} %fusion.128) | copy-start | bytes 6291460
  91.9 10.2 %copy-start.5 = (f32[1024,512]{1,0:T(8,128)S(1)}, f32[1024,512]{1,0:T(8,128)}, u32[]{:S(2)}) copy-start(f32[1024,512]{1,0:T(8,128)} %fusion.130) | copy-start | bytes 6291460
  94.6 5.1 %copy-start.19 = (bf16[1,16,16,128]{3,2,1,0:T(8,128)(2,1)S(1)}, bf16[1,16,16,128]{3,2,1,0:T(8,128)(2,1)}, u32[]{:S(2)}) copy-start(bf16[1,16,16,128]{3,2,1,0:T(8,128)(2,1)} %get-tuple-element.43) | copy-start | bytes 196612
  94.6 5.4 %copy-start.18 = (bf16[1,16,16,128]{3,2,1,0:T(8,128)(2,1)S(1)}, bf16[1,16,16,128]{3,2,1,0:T(8,128)(2,1)}, u32[]{:S(2)}) copy-start(bf16[1,16,16,128]{3,2,1,0:T(8,128)(2,1)} %get-tuple-element.44) | copy-start | bytes 196612
  95.7 2.5 %copy-start.17 = (bf16[1,16,16,128]{3,2,1,0:T(8,128)(2,1)S(1)}, bf16[1,16,16,128]{3,2,1,0:T(8,128)(2,1)}, u32[]{:S(2)}) copy-start(bf16[1,16,16,128]{3,2,1,0:T(8,128)(2,1)} %param.13) | copy-start | bytes 196612
  95.8 6.4 %copy-start.3 = (f32[1024,512]{1,0:T(8,128)S(1)}, f32[1024,512]{1,0:T(8,128)}, u32[]{:S(2)}) copy-start(f32[1024,512]{1,0:T(8,128)} %fusion.127) | copy-start | bytes 6291460
  97.0 5.2 %copy-start.2 = (f32[512,1024]{0,1:T(8,128)S(1)}, f32[512,1024]{0,1:T(8,128)}, u32[]{:S(2)}) copy-start(f32[512,1024]{0,1:T(8,128)} %fusion.126) | copy-start | bytes 6291460
  98.5 3.7 %copy-start.1 = (f32[1024,512]{1,0:T(8,128)S(1)}, f32[1024,512]{1,0:T(8,128)}, u32[]{:S(2)}) copy-start(f32[1024,512]{1,0:T(8,128)} %fusion.125) | copy-start | bytes 6291460
  100.0 2.2 %copy-start = (f32[1024,512]{1,0:T(8,128)S(1)}, f32[1024,512]{1,0:T(8,128)}, u32[]{:S(2)}) copy-start(f32[1024,512]{1,0:T(8,128)} %fusion.124) | copy-start | bytes 6291460
  120.8 1.8 %copy-start.7 = (bf16[8,9,64,128]{3,2,1,0:T(8,128)(2,1)S(1)}, bf16[8,9,64,128]{3,2,1,0:T(8,128)(2,1)}, u32[]{:S(2)}) copy-start(bf16[8,9,64,128]{3,2,1,0:T(8,128)(2,1)} %param.10) | copy-start | bytes 3538948
  122.6 1.3 copy-start.9
Sparse Core Ops, SparseCore 0:
  106.2 61.6 all-reduce.8
